TPU v7x, 32 devices: a whole 2x2x4 slice. The times are simulated.
32 devices in a mesh: comp: 2 (over y), tile: 4 (over x, core), lev: 4 (over z).
Axes of the slice: x: 2, y: 2, z: 4, core: 2. Of those that a mesh axis runs over, the one named last changes fastest.
Arguments:
- thermal_anomaly: float32 [2, 80, 2048], P('comp', 'lev', 'tile'), may hold values from -6 to 6
- right_face_transport_ratio: float32 [2, 80, 2048], P('comp', 'lev', 'tile'), may hold values from -0.45 to 0.45
- species_ratios: float32 [2, 40, 80, 2048], P('comp', None, 'lev', 'tile'), may hold values from 0.1 to 3
- lateral_spreading_number: float32 [2, 80, 2048], P('comp', 'lev', 'tile'), may hold values from 0.05 to 0.2
- depth_physics_operator: float32 [2, 80, 80], P('comp'), may hold values from -1 to 1, as said below
- exchange_weight_table: float32 [2048, 4], P('tile'), may hold values from 0.05 to 0.5
- sky_point_of_entry: int32 [2048, 4], P('tile'), may hold values from 0 to 2047, as said below
- water_indicator: int32 [2048], P('tile'), may hold values 0 or 1
Outputs:
- thermal_anomaly_ending: float32 [2, 80, 2048], P('comp', 'lev', 'tile')
- species_ratios_ending: float32 [2, 40, 80, 2048], P('comp', None, 'lev', 'tile')
Inputs may be any that keep to these rules, and one draw needn't show every extreme that they name: The ocean cells of each block of 512 (cells b * 512 to (b + 1) * 512 - 1) take their sources near the matching cells of one atmosphere block p(b), p a permutation of the blocks: sky_point_of_entry[j, k] lies cyclically within 128 cells of p(b) * 512 + (j mod 512). `depth_physics_operator`: each matrix has diagonal entries between 0.5 and 1.
All inputs are finite; a program needn't handle non-finite values. No bound on the sum of `water_indicator` on one device may be relied on, other than what follows from the above.
Results may differ from a plain program's by a relative error of at most 0.0003.
Values sent between devices are 32-bit elements; how exact they have to be, the bound alone decides.
No kernel may reach another device: no remote copies, remote signals or barrier semaphores. Data moves between devices by JAX's collectives and lax.ppermute only.
A program may use at most 64 MiB of HBM per device.

v0:
```python
import jax
import jax.numpy as jnp
from jax import lax
from jax.sharding import PartitionSpec as P

NFLUX = 4


def extended(x, sides, width):
    for axis, dim in sides:
        devices, length = (lax.axis_size(axis), x.shape[dim])
        up = [(i, (i + 1) % devices) for i in range(devices)]
        down = [(j, i) for i, j in up]
        last = lax.slice_in_dim(x, length - width, length, axis=dim)
        first = lax.slice_in_dim(x, 0, width, axis=dim)
        before = lax.ppermute(last, axis, up)
        after = lax.ppermute(first, axis, down)
        x = jnp.concatenate([before, x, after], axis=dim)
    return x


def passed_along(value, axis, steps):
    count = lax.axis_size(axis)
    first, last = (max(0, -steps), min(count, count - steps))
    return lax.ppermute(value, axis, [(source, source + steps) for source in range(first, last)])


def advance(padded, lateral_spreading_number):
    middle = padded[..., 1:-1]
    before = padded[..., :-2]
    after = padded[..., 2:]
    speed = middle[:, 1:2]
    speed_left = before[:, 1:2]
    flux_right = jnp.maximum(speed, 0.0) * middle + jnp.minimum(speed, 0.0) * after
    flux_left = jnp.maximum(speed_left, 0.0) * before + jnp.minimum(speed_left, 0.0) * middle
    tendency = -(flux_right - flux_left)
    thermal_energy = middle[:, 0]
    heat_next = thermal_energy + (
        tendency[:, 0]
        + lateral_spreading_number * (before[:, 0] - 2.0 * thermal_energy + after[:, 0])
    )
    tracer_next = middle[:, 2:] + tendency[:, 2:]
    return jnp.concatenate([heat_next[:, None], speed, tracer_next], axis=1)


def body(
    thermal_anomaly,
    right_face_transport_ratio,
    species_ratios,
    lateral_spreading_number,
    depth_physics_operator,
    exchange_weight_table,
    sky_point_of_entry,
    water_indicator,
):
    sections = lax.axis_size("comp")
    is_ocean = lax.axis_index("comp") >= sections // 2
    joined_quantities = jnp.concatenate(
        [thermal_anomaly[:, None], right_face_transport_ratio[:, None], species_ratios], axis=1
    )
    for substep in range(2):
        padded = extended(joined_quantities, (("tile", 3),), 1)
        advanced = advance(padded, lateral_spreading_number)
        if substep == 0:
            joined_quantities = advanced
        else:
            joined_quantities = jnp.where(is_ocean, joined_quantities, advanced)
    column = joined_quantities[0, 0]
    level_count = column.shape[0]
    offset = lax.axis_index("lev") * level_count
    matrix = depth_physics_operator[0]
    my_rows = lax.dynamic_slice_in_dim(matrix, offset, level_count, 0)
    blended_profiles = jnp.dot(
        my_rows,
        lax.all_gather(column, "lev", axis=0, tiled=True),
        precision=lax.Precision.HIGHEST,
        preferred_element_type=jnp.float32,
    )
    surface = jnp.concatenate(
        [blended_profiles[0:1], joined_quantities[0, 2 : 2 + NFLUX - 1, 0]], 0
    )
    whole = lax.all_gather(surface, "tile", axis=1, tiled=True)
    received = passed_along(whole, "comp", sections // 2)
    picked = received[:, sky_point_of_entry]
    remapped = jnp.sum(picked * exchange_weight_table, -1)
    updated = surface + 0.5 * (remapped - surface)
    at_sea = jnp.logical_and(
        jnp.logical_and(is_ocean, lax.axis_index("lev") == 0), water_indicator == 1
    )
    renewed_interface_values = jnp.where(at_sea[None, :], updated, surface)
    thermal_anomaly_ending = blended_profiles.at[0].set(renewed_interface_values[0])[None]
    species_ratios_ending = (
        joined_quantities[:, 2:].at[0, 0 : NFLUX - 1, 0].set(renewed_interface_values[1:])
    )
    return (thermal_anomaly_ending, species_ratios_ending)


def solution(mesh):
    in_specs = (
        P("comp", "lev", "tile"),
        P("comp", "lev", "tile"),
        P("comp", None, "lev", "tile"),
        P("comp", "lev", "tile"),
        P("comp", None, None),
        P("tile", None),
        P("tile", None),
        P("tile"),
    )
    out_specs = (P("comp", "lev", "tile"), P("comp", None, "lev", "tile"))
    return jax.shard_map(body, mesh=mesh, in_specs=in_specs, out_specs=out_specs, check_vma=False)
```

profile of v0, /device:TPU:0, one launch (start us, length us, event | category | flops | bytes accessed | tf_op | source)
XLA Modules:
  0.0 121.7 jit_solution(12595853146820664689)
XLA Ops:
  0.7 3.1 %copy.245 = f32[1,40,20,512]{3,0,2,1:T(1,128)S(1)} copy(f32[1,40,20,512]{3,1,2,0:T(8,128)} %param.14) | data formatting | bytes 3276800 | tf_op args[2]
  3.8 2.4 %fusion.8 = f32[1,42,20,512]{3,0,2,1:T(1,128)S(1)} fusion(f32[1,1,20,512]{3,0,2,1:T(1,128)S(1)} %bitcast.89, f32[1,40,20,512]{3,0,2,1:T(1,128)S(1)} %copy.245, f32[1,1,20,512]{3,0,2,1:T(1,128)S(1)} %bitcast.100), kind=kLoop, calls=%fused_computation.17 | loop fusion | flops 860160 | bytes 3440640 | tf_op jit(solution)/shard_map/concatenate | solution.py:58
  6.2 2.1 %fusion.40 = (f32[1,42,20,1]{3,0,2,1:T(1,128)}, f32[1,42,20,1]{3,0,2,1:T(1,128)}) fusion(f32[1,42,20,512]{3,0,2,1:T(1,128)S(1)} %fusion.8), kind=kLoop, calls=%fused_computation.80 | loop fusion | bytes 13440 | tf_op jit(solution)/shard_map/slice | solution.py:15
  8.3 2.4 %collective-permute-start = (f32[1,42,20,1]{3,0,2,1:T(1,128)}, f32[1,42,20,1]{3,0,2,1:T(1,128)S(1)}, u32[]{:S(2)}, u32[]{:S(2)}) collective-permute-start(f32[1,42,20,1]{3,0,2,1:T(1,128)} %get-tuple-element.56), channel_id=1, source_target_pairs={{4,0},{8,4},{12,8},{0,12},{5,1},{9,5},{13,9},{1,13},{6,2},{10,6},{... | collective-permute-start | bytes 10088 | tf_op jit(solution)/shard_map/ppermute | solution.py:17
  10.8 0.6 copy_bitcast_fusion
  11.8 9.5 %collective-permute-done = f32[1,42,20,1]{3,0,2,1:T(1,128)S(1)} collective-permute-done((f32[1,42,20,1]{3,0,2,1:T(1,128)}, f32[1,42,20,1]{3,0,2,1:T(1,128)S(1)}, u32[]{:S(2)}, u32[]{:S(2)}) %collective-permute-start) | collective-permute-done | bytes 3392 | tf_op jit(solution)/shard_map/ppermute | solution.py:17
  21.3 0.9 collective-permute-done.1
  22.3 12.0 %fusion.5 = (f32[1,42,20,513]{3,0,2,1:T(1,128)S(1)}, f32[1,42,20,513]{3,0,2,1:T(1,128)S(1)}) fusion(f32[1,1,20,512]{3,0,2,1:T(1,128)S(1)} %bitcast.90, f32[1,42,20,1]{3,0,2,1:T(1,128)S(1)} %collective-permute-done, f32[1,40,20,512]{3,0,2,1:T(1,128)S(1)} %copy.245, f32[1,1,20,512]{3,0,2,1:T(1,128)S(1)} %bitcast.101, ...), kind=kLoop, calls=%fused_computation.10 | loop fusion | flops 2585520 | bytes 5174400 | tf_op jit(solution)/shard_map/concatenate | solution.py:18
  34.4 4.9 %fusion.17 = f32[1,42,20,512]{3,0,2,1:T(1,128)S(1)} fusion(f32[1,42,20,513]{3,0,2,1:T(1,128)S(1)} %get-tuple-element.55, f32[1,42,20,513]{3,0,2,1:T(1,128)S(1)} %get-tuple-element.54, f32[20,512]{1,0:T(8,128)S(1)} %get-tuple-element.63, f32[20,512]{1,0:T(8,128)S(1)} %get-tuple-element.62, f32[20,512]{1,0:T(8,128)S(1)} %copy-done.5, ...), kind=kLoop, calls=%fused_computation.30 | loop fusion | flops 4300800 | bytes 7045120 | tf_op jit(solution)/shard_map/neg | solution.py:36
  39.3 2.2 %slice_add_fusion.1 = f32[1,40,20,512]{3,0,2,1:T(1,128)S(1)} fusion(f32[1,42,20,512]{3,0,2,1:T(1,128)S(1)} %fusion.17, f32[1,40,20,512]{3,1,2,0:T(8,128)S(1)} %copy-done.2), kind=kLoop, calls=%fused_computation.33 | loop fusion | flops 409600 | bytes 4915200 | tf_op jit(solution)/shard_map/add | solution.py:42
  41.8 2.4 %fusion.9 = f32[1,42,20,512]{3,0,2,1:T(1,128)S(1)} fusion(f32[1,1,20,512]{3,0,2,1:T(1,128)S(1)} %bitcast.92, f32[1,40,20,512]{3,0,2,1:T(1,128)S(1)} %slice_add_fusion.1, f32[1,1,20,512]{3,0,2,1:T(1,128)S(1)} %bitcast.97), kind=kLoop, calls=%fused_computation.18 | loop fusion | flops 860160 | bytes 3440640 | tf_op jit(solution)/shard_map/concatenate | solution.py:43
  44.2 2.1 %fusion.39 = (f32[1,42,20,1]{3,0,2,1:T(1,128)}, f32[1,42,20,1]{3,0,2,1:T(1,128)}) fusion(f32[1,42,20,512]{3,0,2,1:T(1,128)S(1)} %fusion.9), kind=kLoop, calls=%fused_computation.79 | loop fusion | bytes 13440 | tf_op jit(solution)/shard_map/slice | solution.py:15
  46.2 1.2 collective-permute-start.2
  47.4 10.3 %collective-permute-done.2 = f32[1,42,20,1]{3,0,2,1:T(1,128)} collective-permute-done((f32[1,42,20,1]{3,0,2,1:T(1,128)}, f32[1,42,20,1]{3,0,2,1:T(1,128)}, u32[]{:S(2)}, u32[]{:S(2)}) %collective-permute-start.2) | collective-permute-done | bytes 3392 | tf_op jit(solution)/shard_map/ppermute | solution.py:17
  57.7 1.0 collective-permute-done.3
  58.7 13.0 %fusion.7 = (f32[1,42,20,513]{3,0,2,1:T(1,128)S(1)}, f32[1,42,20,513]{3,0,2,1:T(1,128)S(1)}) fusion(f32[1,1,20,512]{3,0,2,1:T(1,128)S(1)} %bitcast.93, f32[1,42,20,1]{3,0,2,1:T(1,128)} %collective-permute-done.2, f32[1,40,20,512]{3,0,2,1:T(1,128)S(1)} %slice_add_fusion.1, f32[1,1,20,512]{3,0,2,1:T(1,128)S(1)} %bitcast.98, ...), kind=kLoop, calls=%fused_computation.12 | loop fusion | flops 2585520 | bytes 5174400 | tf_op jit(solution)/shard_map/concatenate | solution.py:18
  71.9 4.9 %fusion.18 = f32[1,42,20,512]{3,0,2,1:T(1,128)S(1)} fusion(f32[1,42,20,513]{3,0,2,1:T(1,128)S(1)} %get-tuple-element.51, f32[1,42,20,513]{3,0,2,1:T(1,128)S(1)} %get-tuple-element.50, f32[20,512]{1,0:T(8,128)S(1)} %get-tuple-element.59, f32[20,512]{1,0:T(8,128)S(1)} %get-tuple-element.58, f32[20,512]{1,0:T(8,128)S(1)} %copy-done.6, ...), kind=kLoop, calls=%fused_computation.31 | loop fusion | flops 4300800 | bytes 7045120 | tf_op jit(solution)/shard_map/neg | solution.py:36
  76.8 0.2 add_bitcast_fusion
  77.0 3.3 %slice_add_fusion = f32[1,40,20,512]{3,0,2,1:T(1,128)S(1)} fusion(f32[1,40,20,512]{3,0,2,1:T(1,128)S(1)} %slice_add_fusion.1, f32[1,42,20,512]{3,0,2,1:T(1,128)S(1)} %fusion.18), kind=kLoop, calls=%fused_computation.32 | loop fusion | flops 409600 | bytes 4915200 | tf_op jit(solution)/shard_map/add | solution.py:42
  80.3 2.4 %fusion.10 = f32[1,42,20,512]{3,0,2,1:T(1,128)S(1)} fusion(f32[1,1,20,512]{3,0,2,1:T(1,128)S(1)} %bitcast.95, f32[1,40,20,512]{3,0,2,1:T(1,128)S(1)} %slice_add_fusion, f32[1,1,20,512]{3,0,2,1:T(1,128)S(1)} %add_bitcast_fusion), kind=kLoop, calls=%fused_computation.19 | loop fusion | flops 860160 | bytes 3440640 | tf_op jit(solution)/shard_map/concatenate | solution.py:43
  82.7 1.0 copy_select_fusion
  83.8 1.2 %copy-done.1 = f32[1,42,20,512]{3,1,0,2:T(8,128)} copy-done((f32[1,42,20,512]{3,1,0,2:T(8,128)}, f32[1,42,20,512]{3,1,0,2:T(8,128)S(1)}, u32[]{:S(2)}) %copy-start.1) | copy-done | bytes 1720344
  85.0 13.7 %all-gather = f32[1,1,80,512]{3,1,0,2:T(1,128)S(1)} all-gather(f32[1,1,20,512]{3,1,0,2:T(1,128)S(1)} %slice.171), channel_id=2, replica_groups=mesh['comp'=2,'tile'=4,'lev'=4] {'lev'}, dimensions={2}, use_global_device_ids=true | all-gather | bytes 204800 | tf_op jit(solution)/shard_map/all_gather | solution.py:75
  98.8 0.2 fusion.19
  99.0 5.2 %all_gather.7 = f32[4,2048]{1,0:T(4,128)S(1)} all-gather(f32[4,512]{1,0:T(4,128)S(1)} %pad_maximum_fusion.7), channel_id=1, replica_groups=mesh['comp'=2,'tile'=4,'lev'=4] {'tile'}, dimensions={1}, use_global_device_ids=true | all-gather | bytes 40960 | tf_op jit(solution)/shard_map/all_gather | solution.py:82
  104.2 3.4 %collective-permute-start.4 = (f32[4,2048]{1,0:T(4,128)S(1)}, f32[4,2048]{1,0:T(4,128)S(1)}, u32[]{:S(2)}, u32[]{:S(2)}) collective-permute-start(f32[4,2048]{1,0:T(4,128)S(1)} %all_gather.7), channel_id=1, source_target_pairs={{0,16},{1,17},{2,18},{3,19},{4,20},{5,21},{6,22},{7,23},{8,24},{9,... | collective-permute-start | bytes 98312 | tf_op jit(solution)/shard_map/ppermute | solution.py:25
  107.8 3.0 %slice.175 = f32[1,40,20,512]{3,1,0,2:T(8,128)} slice(f32[1,42,20,512]{3,1,0,2:T(8,128)} %copy-done.1), slice={[0:1], [2:42], [0:20], [0:512]} | slice | bytes 3276800 | tf_op jit(solution)/shard_map/slice | solution.py:93
  110.8 0.4 copy.252
  111.2 5.5 %gather_fusion = f32[2048,4]{1,0:T(8,128)S(1)} fusion(f32[4,2048]{0,1:T(8,128)S(1)} %copy.252, s32[2048]{0:T(1024)S(1)} %broadcast_clamp_fusion), kind=kCustom, calls=%fused_computation | custom fusion | bytes 73728 | tf_op jit(solution)/shard_map/gather | solution.py:84
  116.7 2.8 %multiply_reduce_fusion = f32[512,4]{1,0:T(8,128)S(1)} fusion(f32[512,4,4]{2,1,0:T(4,128)S(1)} %bitcast.88, f32[512,4]{1,0:T(8,128)S(1)} %copy.253), kind=kLoop, calls=%fused_computation.34 | loop fusion | flops 14336 | bytes 49152 | tf_op jit(solution)/shard_map/reduce_sum | solution.py:85
  119.7 0.7 copy.256
  120.4 1.4 %scatter.9 = f32[1,40,20,512]{3,1,0,2:T(8,128)} dynamic-update-slice(f32[1,40,20,512]{3,1,0,2:T(8,128)} %slice.175, f32[1,3,1,512]{3,1,0,2:T(4,128)S(1)} %slice_bitcast_fusion.6, s32[]{:T(128)} %constant.77.clone.1, s32[]{:T(128)} %constant.77.clone.1, s32[]{:T(128)} %constant.77.clone.1, s32[]{:T(128)} %constant.77.clone.1) | dynamic-update-slice | bytes 12292 | tf_op jit(solution)/shard_map/scatter | solution.py:93
  (51 shorter events, 1.1 us)
Async XLA Ops:
  0.6 98.1 %copy-start = (f32[1,80,80]{2,1,0:T(8,128)S(1)}, f32[1,80,80]{2,1,0:T(8,128)}, u32[]{:S(2)}) copy-start(f32[1,80,80]{2,1,0:T(8,128)} %param.16) | copy-start | bytes 76804
  0.6 3.2 %copy-start.3 = (f32[1,20,512]{2,0,1:T(1,128)S(1)}, f32[1,20,512]{2,0,1:T(1,128)}, u32[]{:S(2)}) copy-start(f32[1,20,512]{2,0,1:T(1,128)} %param.13) | copy-start | bytes 122884
  0.7 3.2 %copy-start.4 = (f32[1,20,512]{2,0,1:T(1,128)S(1)}, f32[1,20,512]{2,0,1:T(1,128)}, u32[]{:S(2)}) copy-start(f32[1,20,512]{2,0,1:T(1,128)} %param.12) | copy-start | bytes 122884
  6.2 5.2 %copy-start.12 = (s32[512,4]{0,1:T(4,128)S(1)}, s32[512,4]{0,1:T(4,128)}, u32[]{:S(2)}) copy-start(s32[512,4]{0,1:T(4,128)} %param.18) | copy-start | bytes 24580
  8.3 13.0 %collective-permute-start = (f32[1,42,20,1]{3,0,2,1:T(1,128)}, f32[1,42,20,1]{3,0,2,1:T(1,128)S(1)}, u32[]{:S(2)}, u32[]{:S(2)}) collective-permute-start(f32[1,42,20,1]{3,0,2,1:T(1,128)} %get-tuple-element.56), channel_id=1, source_target_pairs={{4,0},{8,4},{12,8},{0,12},{5,1},{9,5},{13,9},{1,13},{6,2},{10,6},{... | collective-permute-start | bytes 10088 | tf_op jit(solution)/shard_map/ppermute | solution.py:17
  10.7 11.5 %collective-permute-start.1 = (f32[1,42,20,1]{3,0,2,1:T(1,128)}, f32[1,42,20,1]{3,0,2,1:T(1,128)S(1)}, u32[]{:S(2)}, u32[]{:S(2)}) collective-permute-start(f32[1,42,20,1]{3,0,2,1:T(1,128)} %get-tuple-element.57), channel_id=1, source_target_pairs={{0,4},{4,8},{8,12},{12,0},{1,5},{5,9},{9,13},{13,1},{2,6},{6,10},{... | collective-permute-start | bytes 10088 | tf_op jit(solution)/shard_map/ppermute | solution.py:16
  11.8 22.6 %copy-start.5 = (f32[20,512]{1,0:T(8,128)S(1)}, f32[20,512]{1,0:T(8,128)}, u32[]{:S(2)}) copy-start(f32[20,512]{1,0:T(8,128)} %get-tuple-element.64) | copy-start | bytes 122884
  11.8 22.6 %copy-start.7 = (f32[20,512]{1,0:T(8,128)S(1)}, f32[20,512]{1,0:T(8,128)}, u32[]{:S(2)}) copy-start(f32[20,512]{1,0:T(8,128)} %get-tuple-element.65) | copy-start | bytes 122884
  34.4 4.9 %copy-start.2 = (f32[1,40,20,512]{3,1,2,0:T(8,128)S(1)}, f32[1,40,20,512]{3,1,2,0:T(8,128)}, u32[]{:S(2)}) copy-start(f32[1,40,20,512]{3,1,2,0:T(8,128)} %param.14) | copy-start | bytes 4915204
  39.3 2.3 %copy-start.9 = (f32[1,20,512]{2,0,1:T(1,128)S(1)}, f32[1,20,512]{2,0,1:T(1,128)}, u32[]{:S(2)}) copy-start(f32[1,20,512]{2,0,1:T(1,128)} %param.15) | copy-start | bytes 122884
  46.2 11.5 %collective-permute-start.2 = (f32[1,42,20,1]{3,0,2,1:T(1,128)}, f32[1,42,20,1]{3,0,2,1:T(1,128)}, u32[]{:S(2)}, u32[]{:S(2)}) collective-permute-start(f32[1,42,20,1]{3,0,2,1:T(1,128)} %get-tuple-element.52), channel_id=1, source_target_pairs={{4,0},{8,4},{12,8},{0,12},{5,1},{9,5},{13,9},{1,13},{6,2},{10,6},{... | collective-permute-start | bytes 10088 | tf_op jit(solution)/shard_map/ppermute | solution.py:17
  47.4 11.3 %collective-permute-start.3 = (f32[1,42,20,1]{3,0,2,1:T(1,128)}, f32[1,42,20,1]{3,0,2,1:T(1,128)}, u32[]{:S(2)}, u32[]{:S(2)}) collective-permute-start(f32[1,42,20,1]{3,0,2,1:T(1,128)} %get-tuple-element.53), channel_id=1, source_target_pairs={{0,4},{4,8},{8,12},{12,0},{1,5},{5,9},{9,13},{13,1},{2,6},{6,10},{... | collective-permute-start | bytes 10088 | tf_op jit(solution)/shard_map/ppermute | solution.py:16
  47.4 24.4 %copy-start.6 = (f32[20,512]{1,0:T(8,128)S(1)}, f32[20,512]{1,0:T(8,128)}, u32[]{:S(2)}) copy-start(f32[20,512]{1,0:T(8,128)} %get-tuple-element.64) | copy-start | bytes 122884
  47.4 24.4 %copy-start.8 = (f32[20,512]{1,0:T(8,128)S(1)}, f32[20,512]{1,0:T(8,128)}, u32[]{:S(2)}) copy-start(f32[20,512]{1,0:T(8,128)} %get-tuple-element.65) | copy-start | bytes 122884
  71.8 4.9 %copy-start.10 = (f32[1,20,512]{2,0,1:T(1,128)S(1)}, f32[1,20,512]{2,0,1:T(1,128)}, u32[]{:S(2)}) copy-start(f32[1,20,512]{2,0,1:T(1,128)} %param.15) | copy-start | bytes 122884
  82.7 24.9 %copy-start.13 = (s32[512]{0:T(512)S(1)}, s32[512]{0:T(512)}, u32[]{:S(2)}) copy-start(s32[512]{0:T(512)} %param.19) | copy-start | bytes 6148
  82.7 24.9 %copy-start.11 = (f32[512,4]{0,1:T(4,128)S(1)}, f32[512,4]{0,1:T(4,128)}, u32[]{:S(2)}) copy-start(f32[512,4]{0,1:T(4,128)} %param.17) | copy-start | bytes 24580
  83.7 1.3 %copy-start.1 = (f32[1,42,20,512]{3,1,0,2:T(8,128)}, f32[1,42,20,512]{3,1,0,2:T(8,128)S(1)}, u32[]{:S(2)}) copy-start(f32[1,42,20,512]{3,1,0,2:T(8,128)S(1)} %copy_select_fusion) | copy-start | bytes 5160964
  104.2 6.6 %collective-permute-start.4 = (f32[4,2048]{1,0:T(4,128)S(1)}, f32[4,2048]{1,0:T(4,128)S(1)}, u32[]{:S(2)}, u32[]{:S(2)}) collective-permute-start(f32[4,2048]{1,0:T(4,128)S(1)} %all_gather.7), channel_id=1, source_target_pairs={{0,16},{1,17},{2,18},{3,19},{4,20},{5,21},{6,22},{7,23},{8,24},{9,... | collective-permute-start | bytes 98312 | tf_op jit(solution)/shard_map/ppermute | solution.py:25
where the time goes:
time: 122 us
  other arithmetic  52 us (43%)
  waiting for transfers between devices  21.8 us (18%)
  local copies, waits for them, and re-layouts  20.8 us (17%)
  blocking collectives  18.9 us (15%)
  starting transfers between devices  6.99 us (6%)
    concatenate x2, other arithmetic, extended(): x = jnp.concatenate([before, x, after], axis=dim)  25.1 us
    ppermute x2, waiting for transfers between devices, extended(): after = lax.ppermute(first, axis, down)  19.8 us
    all_gather x1, blocking collectives, body(): lax.all_gather(column, 'lev', axis=0, tiled=True)  13.7 us
    neg x2, other arithmetic, advance(): tendency = -(flux_right - flux_left)  9.84 us
    unnamed x32, local copies, waits for them, and re-layouts  5.92 us
    add x2, other arithmetic, advance(): tracer_next = middle[:, 2:] + tendency[:, 2:]  5.57 us
    gather x1, local copies, waits for them, and re-layouts, body(): picked = received[:, sky_point_of_entry]  5.48 us
    all_gather x1, blocking collectives, body(): whole = lax.all_gather(surface, 'tile', axis=1, tiled=True)  5.19 us
  transfers between devices with their start and end apart: 5, of which 4 were waited for; matrix products, arithmetic and copies ran while one was open for 3% of the time, Pallas kernels for 0%

commit v1 on v0

--- a/solution.py
+++ b/solution.py
@@ -4,6 +4,18 @@
 from jax.sharding import PartitionSpec as P
 
 NFLUX = 4
+
+
+def doubled_up(x, axis, dim):
+    ways, here = (lax.axis_size(axis), lax.axis_index(axis))
+    grown, reach = (x, 1)
+    while reach < ways:
+        theirs = lax.ppermute(grown, axis, [(d, d ^ reach) for d in range(ways)])
+        mine_first = jnp.concatenate([grown, theirs], axis=dim)
+        theirs_first = jnp.concatenate([theirs, grown], axis=dim)
+        grown = jnp.where(here & reach == 0, mine_first, theirs_first)
+        reach = 2 * reach
+    return grown
 
 
 def extended(x, sides, width):
@@ -72,7 +84,7 @@
     my_rows = lax.dynamic_slice_in_dim(matrix, offset, level_count, 0)
     blended_profiles = jnp.dot(
         my_rows,
-        lax.all_gather(column, "lev", axis=0, tiled=True),
+        doubled_up(column, "lev", 0),
         precision=lax.Precision.HIGHEST,
         preferred_element_type=jnp.float32,
     )

time: 122 us -> 119 us (0.975)
  blocking collectives: 18.9 us -> 5.19 us
  waiting for transfers between devices: 21.8 us -> 28.1 us
  starting transfers between devices: 6.99 us -> 11.2 us
    all_gather x1 -> x0, blocking collectives: 13.7 us -> none  [body(): lax.all_gather(column, 'lev', axis=0, tiled=True)]
    ppermute x0 -> x2, starting transfers between devices: none -> 4.23 us  [doubled_up(): theirs = lax.ppermute(grown, axis, [(d, d ^ reach) for d in range(ways)])]
    ppermute x0 -> x2, waiting for transfers between devices: none -> 4.12 us  [doubled_up(): theirs = lax.ppermute(grown, axis, [(d, d ^ reach) for d in range(ways)])]
    slice x1 -> x2, local copies, waits for them, and re-layouts: 3.01 us -> 0.01 us  [body(): joined_quantities[:, 2:].at[0, 0:NFLUX - 1, 0]]
    gather x1, local copies, waits for them, and re-layouts: 5.48 us -> 7.64 us  [body(): picked = received[:, sky_point_of_entry]]
    unnamed x32 -> x30, local copies, waits for them, and re-layouts: 5.92 us -> 7.47 us
    ppermute x1, waiting for transfers between devices: 0.01 us -> 1.39 us  [passed_along(): lax.ppermute(value, axis, [(source, source + steps) for source in range(f...]
    scatter x1, local copies, waits for them, and re-layouts: 1.36 us -> 0.09 us  [body(): joined_quantities[:, 2:].at[0, 0:NFLUX - 1, 0]]
  transfers between devices with their start and end apart: 5 -> 7, of which waited for: 4 -> 7; matrix products, arithmetic and copies ran while one was open for 3% -> 1% of each run, Pallas kernels for 0% -> 0%
where the time goes in v1:
time: 119 us; the launch traced here: 118 us
  other arithmetic  52.5 us (44%)
  waiting for transfers between devices  28.1 us (24%)
  local copies, waits for them, and re-layouts  20.1 us (17%)
  starting transfers between devices  11.2 us (9%)
  blocking collectives  5.19 us (4%)
    concatenate x2, other arithmetic, extended(): x = jnp.concatenate([before, x, after], axis=dim)  25.1 us
    ppermute x2, waiting for transfers between devices, extended(): after = lax.ppermute(first, axis, down)  20.5 us
    neg x2, other arithmetic, advance(): tendency = -(flux_right - flux_left)  9.87 us
    gather x1, local copies, waits for them, and re-layouts, body(): picked = received[:, sky_point_of_entry]  7.64 us
    unnamed x30, local copies, waits for them, and re-layouts  7.47 us
    add x2, other arithmetic, advance(): tracer_next = middle[:, 2:] + tendency[:, 2:]  5.57 us
    all_gather x1, blocking collectives, body(): whole = lax.all_gather(surface, 'tile', axis=1, tiled=True)  5.19 us
    concatenate x3, other arithmetic, advance(): return jnp.concatenate([heat_next[:, None], speed, tracer_next], axis=1)  4.97 us
  transfers between devices with their start and end apart: 7, of which 7 were waited for; matrix products, arithmetic and copies ran while one was open for 1% of the time, Pallas kernels for 0%

profile of v1, /device:TPU:0, one launch (start us, length us, event | category | flops | bytes accessed | tf_op | source)
XLA Modules:
  0.0 118.5 jit_solution(12082512445517099014)
XLA Ops:
  0.7 3.1 %copy.245 = f32[1,40,20,512]{3,0,2,1:T(1,128)S(1)} copy(f32[1,40,20,512]{3,1,2,0:T(8,128)} %param.14) | data formatting | bytes 3276800 | tf_op args[2]
  3.8 2.4 %fusion.8 = f32[1,42,20,512]{3,0,2,1:T(1,128)S(1)} fusion(f32[1,1,20,512]{3,0,2,1:T(1,128)S(1)} %bitcast.86, f32[1,40,20,512]{3,0,2,1:T(1,128)S(1)} %copy.245, f32[1,1,20,512]{3,0,2,1:T(1,128)S(1)} %bitcast.96), kind=kLoop, calls=%fused_computation.17 | loop fusion | flops 860160 | bytes 3440640 | tf_op jit(solution)/shard_map/concatenate | solution.py:70
  6.2 1.2 fusion.45
  7.4 2.5 %collective-permute-start = (f32[1,42,20,1]{3,0,2,1:T(1,128)S(1)}, f32[1,42,20,1]{3,0,2,1:T(1,128)S(1)}, u32[]{:S(2)}, u32[]{:S(2)}) collective-permute-start(f32[1,42,20,1]{3,0,2,1:T(1,128)S(1)} %get-tuple-element.56), channel_id=1, source_target_pairs={{4,0},{8,4},{12,8},{0,12},{5,1},{9,5},{13,9},{1,13},{6,2},{10,6},{... | collective-permute-start | bytes 10088 | tf_op jit(solution)/shard_map/ppermute | solution.py:29
  10.0 10.2 %collective-permute-done = f32[1,42,20,1]{3,0,2,1:T(1,128)S(1)} collective-permute-done((f32[1,42,20,1]{3,0,2,1:T(1,128)S(1)}, f32[1,42,20,1]{3,0,2,1:T(1,128)S(1)}, u32[]{:S(2)}, u32[]{:S(2)}) %collective-permute-start) | collective-permute-done | bytes 3392 | tf_op jit(solution)/shard_map/ppermute | solution.py:29
  20.1 1.1 collective-permute-done.1
  21.2 12.0 %fusion.5 = (f32[1,42,20,513]{3,0,2,1:T(1,128)S(1)}, f32[1,42,20,513]{3,0,2,1:T(1,128)S(1)}) fusion(f32[1,1,20,512]{3,0,2,1:T(1,128)S(1)} %bitcast.87, f32[1,42,20,1]{3,0,2,1:T(1,128)S(1)} %collective-permute-done, f32[1,40,20,512]{3,0,2,1:T(1,128)S(1)} %copy.245, f32[1,1,20,512]{3,0,2,1:T(1,128)S(1)} %bitcast.97, f32[1,42,20,1]{3,0,2,1:T(1,128)S(1)} %collective-permute-done.1), kind=kLoop, calls=%fused_computation.10 | loop fusion | flops 2585520 | bytes 5174400 | tf_op jit(solution)/shard_map/concatenate | solution.py:30
  33.3 4.9 %fusion.17 = f32[1,42,20,512]{3,0,2,1:T(1,128)S(1)} fusion(f32[1,42,20,513]{3,0,2,1:T(1,128)S(1)} %get-tuple-element.55, f32[1,42,20,513]{3,0,2,1:T(1,128)S(1)} %get-tuple-element.54, f32[20,512]{1,0:T(8,128)S(1)} %get-tuple-element.63, f32[20,512]{1,0:T(8,128)S(1)} %get-tuple-element.62, f32[20,512]{1,0:T(8,128)S(1)} %get-tuple-element.64, ...), kind=kLoop, calls=%fused_computation.30 | loop fusion | flops 4300800 | bytes 7045120 | tf_op jit(solution)/shard_map/neg | solution.py:48
  38.3 2.2 %slice_add_fusion.1 = f32[1,40,20,512]{3,0,2,1:T(1,128)S(1)} fusion(f32[1,42,20,512]{3,0,2,1:T(1,128)S(1)} %fusion.17, f32[1,40,20,512]{3,1,2,0:T(8,128)S(1)} %copy-done.2), kind=kLoop, calls=%fused_computation.33 | loop fusion | flops 409600 | bytes 4915200 | tf_op jit(solution)/shard_map/add | solution.py:54
  40.7 2.4 %fusion.9 = f32[1,42,20,512]{3,0,2,1:T(1,128)S(1)} fusion(f32[1,1,20,512]{3,0,2,1:T(1,128)S(1)} %bitcast.89, f32[1,40,20,512]{3,0,2,1:T(1,128)S(1)} %slice_add_fusion.1, f32[1,1,20,512]{3,0,2,1:T(1,128)S(1)} %bitcast.93), kind=kLoop, calls=%fused_computation.18 | loop fusion | flops 860160 | bytes 3440640 | tf_op jit(solution)/shard_map/concatenate | solution.py:55
  43.1 2.1 %fusion.44 = (f32[1,42,20,1]{3,0,2,1:T(1,128)}, f32[1,42,20,1]{3,0,2,1:T(1,128)}) fusion(f32[1,42,20,512]{3,0,2,1:T(1,128)S(1)} %fusion.9), kind=kLoop, calls=%fused_computation.87 | loop fusion | bytes 13440 | tf_op jit(solution)/shard_map/slice | solution.py:27
  45.2 1.1 collective-permute-start.2
  46.3 10.4 %collective-permute-done.2 = f32[1,42,20,1]{3,0,2,1:T(1,128)} collective-permute-done((f32[1,42,20,1]{3,0,2,1:T(1,128)}, f32[1,42,20,1]{3,0,2,1:T(1,128)}, u32[]{:S(2)}, u32[]{:S(2)}) %collective-permute-start.2) | collective-permute-done | bytes 3392 | tf_op jit(solution)/shard_map/ppermute | solution.py:29
  56.7 1.0 collective-permute-done.3
  57.7 13.0 %fusion.7 = (f32[1,42,20,513]{3,0,2,1:T(1,128)S(1)}, f32[1,42,20,513]{3,0,2,1:T(1,128)S(1)}) fusion(f32[1,1,20,512]{3,0,2,1:T(1,128)S(1)} %bitcast.90, f32[1,42,20,1]{3,0,2,1:T(1,128)} %collective-permute-done.2, f32[1,40,20,512]{3,0,2,1:T(1,128)S(1)} %slice_add_fusion.1, f32[1,1,20,512]{3,0,2,1:T(1,128)S(1)} %bitcast.94, ...), kind=kLoop, calls=%fused_computation.12 | loop fusion | flops 2585520 | bytes 5174400 | tf_op jit(solution)/shard_map/concatenate | solution.py:30
  70.8 4.9 %fusion.18 = f32[1,42,20,512]{3,0,2,1:T(1,128)S(1)} fusion(f32[1,42,20,513]{3,0,2,1:T(1,128)S(1)} %get-tuple-element.51, f32[1,42,20,513]{3,0,2,1:T(1,128)S(1)} %get-tuple-element.50, f32[20,512]{1,0:T(8,128)S(1)} %get-tuple-element.59, f32[20,512]{1,0:T(8,128)S(1)} %get-tuple-element.58, f32[20,512]{1,0:T(8,128)S(1)} %get-tuple-element.64, ...), kind=kLoop, calls=%fused_computation.31 | loop fusion | flops 4300800 | bytes 7045120 | tf_op jit(solution)/shard_map/neg | solution.py:48
  75.9 3.3 %slice_add_fusion = f32[1,40,20,512]{3,0,2,1:T(1,128)S(1)} fusion(f32[1,40,20,512]{3,0,2,1:T(1,128)S(1)} %slice_add_fusion.1, f32[1,42,20,512]{3,0,2,1:T(1,128)S(1)} %fusion.18), kind=kLoop, calls=%fused_computation.32 | loop fusion | flops 409600 | bytes 4915200 | tf_op jit(solution)/shard_map/add | solution.py:54
  79.3 2.4 %fusion.10 = f32[1,42,20,512]{3,0,2,1:T(1,128)S(1)} fusion(f32[1,1,20,512]{3,0,2,1:T(1,128)S(1)} %bitcast.92, f32[1,40,20,512]{3,0,2,1:T(1,128)S(1)} %slice_add_fusion, f32[1,1,20,512]{3,0,2,1:T(1,128)S(1)} %add_bitcast_fusion), kind=kLoop, calls=%fused_computation.19 | loop fusion | flops 860160 | bytes 3440640 | tf_op jit(solution)/shard_map/concatenate | solution.py:55
  81.7 0.5 copy_select_fusion
  82.2 1.3 %copy-done.1 = f32[1,42,20,512]{3,2,1,0:T(8,128)} copy-done((f32[1,42,20,512]{3,2,1,0:T(8,128)}, f32[1,42,20,512]{3,2,1,0:T(8,128)S(1)}, u32[]{:S(2)}) %copy-start.1) | copy-done | bytes 1720344
  83.5 1.6 %collective-permute-start.4 = (f32[20,512]{1,0:T(8,128)S(1)}, f32[20,512]{1,0:T(8,128)S(1)}, u32[]{:S(2)}, u32[]{:S(2)}) collective-permute-start(f32[20,512]{1,0:T(8,128)S(1)} %slice_bitcast_fusion), channel_id=1, source_target_pairs={{0,1},{1,0},{2,3},{3,2},{4,5},{5,4},{6,7},{7,6},{8,9},{9,8},{10,11... | collective-permute-start | bytes 122888 | tf_op jit(solution)/shard_map/ppermute | solution.py:13
  85.5 2.2 %collective-permute-done.4 = f32[20,512]{1,0:T(8,128)S(1)} collective-permute-done((f32[20,512]{1,0:T(8,128)S(1)}, f32[20,512]{1,0:T(8,128)S(1)}, u32[]{:S(2)}, u32[]{:S(2)}) %collective-permute-start.4) | collective-permute-done | bytes 40992 | tf_op jit(solution)/shard_map/ppermute | solution.py:13
  87.7 2.7 %collective-permute-start.5 = (f32[40,512]{1,0:T(8,128)S(1)}, f32[40,512]{1,0:T(8,128)S(1)}, u32[]{:S(2)}, u32[]{:S(2)}) collective-permute-start(f32[40,512]{1,0:T(8,128)S(1)} %maximum_select_fusion.2), channel_id=1, source_target_pairs={{0,2},{1,3},{2,0},{3,1},{4,6},{5,7},{6,4},{7,5},{8,10},{9,11},{10,... | collective-permute-start | bytes 245768 | tf_op jit(solution)/shard_map/ppermute | solution.py:13
  90.3 0.8 slice.173
  91.1 1.9 %collective-permute-done.5 = f32[40,512]{1,0:T(8,128)S(1)} collective-permute-done((f32[40,512]{1,0:T(8,128)S(1)}, f32[40,512]{1,0:T(8,128)S(1)}, u32[]{:S(2)}, u32[]{:S(2)}) %collective-permute-start.5) | collective-permute-done | bytes 81952 | tf_op jit(solution)/shard_map/ppermute | solution.py:13
  93.3 5.2 %all_gather.3 = f32[4,2048]{1,0:T(4,128)S(1)} all-gather(f32[4,512]{1,0:T(4,128)S(1)} %pad_maximum_fusion.7), channel_id=1, replica_groups=mesh['comp'=2,'tile'=4,'lev'=4] {'tile'}, dimensions={1}, use_global_device_ids=true | all-gather | bytes 40960 | tf_op jit(solution)/shard_map/all_gather | solution.py:94
  98.5 3.4 %collective-permute-start.6 = (f32[4,2048]{1,0:T(4,128)S(1)}, f32[4,2048]{1,0:T(4,128)S(1)}, u32[]{:S(2)}, u32[]{:S(2)}) collective-permute-start(f32[4,2048]{1,0:T(4,128)S(1)} %all_gather.3), channel_id=1, source_target_pairs={{0,16},{1,17},{2,18},{3,19},{4,20},{5,21},{6,22},{7,23},{8,24},{9,... | collective-permute-start | bytes 98312 | tf_op jit(solution)/shard_map/ppermute | solution.py:37
  102.1 1.4 %collective-permute-done.6 = f32[4,2048]{1,0:T(4,128)S(1)} collective-permute-done((f32[4,2048]{1,0:T(4,128)S(1)}, f32[4,2048]{1,0:T(4,128)S(1)}, u32[]{:S(2)}, u32[]{:S(2)}) %collective-permute-start.6) | collective-permute-done | bytes 32800 | tf_op jit(solution)/shard_map/ppermute | solution.py:37
  103.9 7.6 %gather_fusion = f32[2048,4]{1,0:T(8,128)} fusion(f32[4,2048]{0,1:T(8,128)S(1)} %copy.252, s32[2048]{0:T(1024)S(1)} %broadcast_clamp_fusion), kind=kCustom, calls=%fused_computation | custom fusion | bytes 73728 | tf_op jit(solution)/shard_map/gather | solution.py:96
  111.5 3.8 %multiply_reduce_fusion = f32[512,4]{1,0:T(8,128)S(1)} fusion(f32[512,4,4]{2,1,0:T(4,128)} %bitcast.85, f32[512,4]{1,0:T(8,128)S(1)} %copy.253), kind=kLoop, calls=%fused_computation.34 | loop fusion | flops 14336 | bytes 49152 | tf_op jit(solution)/shard_map/reduce_sum | solution.py:97
  115.6 2.1 %copy.257 = f32[1,40,20,512]{3,1,2,0:T(8,128)} copy(f32[1,40,20,512]{3,2,1,0:T(8,128)S(1)} %scatter.9) | data formatting | bytes 3276800
  117.8 0.7 copy.256
  (55 shorter events, 1.9 us)
Async XLA Ops:
  0.6 92.4 %copy-start = (f32[1,80,80]{2,1,0:T(8,128)S(1)}, f32[1,80,80]{2,1,0:T(8,128)}, u32[]{:S(2)}) copy-start(f32[1,80,80]{2,1,0:T(8,128)} %param.16) | copy-start | bytes 76804
  0.6 3.2 %copy-start.3 = (f32[1,20,512]{2,0,1:T(1,128)S(1)}, f32[1,20,512]{2,0,1:T(1,128)}, u32[]{:S(2)}) copy-start(f32[1,20,512]{2,0,1:T(1,128)} %param.13) | copy-start | bytes 122884
  0.7 3.2 %copy-start.4 = (f32[1,20,512]{2,0,1:T(1,128)S(1)}, f32[1,20,512]{2,0,1:T(1,128)}, u32[]{:S(2)}) copy-start(f32[1,20,512]{2,0,1:T(1,128)} %param.12) | copy-start | bytes 122884
  7.4 12.7 %collective-permute-start = (f32[1,42,20,1]{3,0,2,1:T(1,128)S(1)}, f32[1,42,20,1]{3,0,2,1:T(1,128)S(1)}, u32[]{:S(2)}, u32[]{:S(2)}) collective-permute-start(f32[1,42,20,1]{3,0,2,1:T(1,128)S(1)} %get-tuple-element.56), channel_id=1, source_target_pairs={{4,0},{8,4},{12,8},{0,12},{5,1},{9,5},{13,9},{1,13},{6,2},{10,6},{... | collective-permute-start | bytes 10088 | tf_op jit(solution)/shard_map/ppermute | solution.py:29
  9.9 11.3 %collective-permute-start.1 = (f32[1,42,20,1]{3,0,2,1:T(1,128)S(1)}, f32[1,42,20,1]{3,0,2,1:T(1,128)S(1)}, u32[]{:S(2)}, u32[]{:S(2)}) collective-permute-start(f32[1,42,20,1]{3,0,2,1:T(1,128)S(1)} %get-tuple-element.57), channel_id=1, source_target_pairs={{0,4},{4,8},{8,12},{12,0},{1,5},{5,9},{9,13},{13,1},{2,6},{6,10},{... | collective-permute-start | bytes 10088 | tf_op jit(solution)/shard_map/ppermute | solution.py:28
  9.9 23.3 %copy-start.5 = (f32[20,512]{1,0:T(8,128)}, f32[20,512]{1,0:T(8,128)S(1)}, u32[]{:S(2)}) copy-start(f32[20,512]{1,0:T(8,128)S(1)} %get-tuple-element.65) | copy-start | bytes 122884
  33.3 5.0 %copy-start.2 = (f32[1,40,20,512]{3,1,2,0:T(8,128)S(1)}, f32[1,40,20,512]{3,1,2,0:T(8,128)}, u32[]{:S(2)}) copy-start(f32[1,40,20,512]{3,1,2,0:T(8,128)} %param.14) | copy-start | bytes 4915204
  38.3 2.3 %copy-start.7 = (f32[1,20,512]{2,0,1:T(1,128)S(1)}, f32[1,20,512]{2,0,1:T(1,128)}, u32[]{:S(2)}) copy-start(f32[1,20,512]{2,0,1:T(1,128)} %param.15) | copy-start | bytes 122884
  45.2 11.5 %collective-permute-start.2 = (f32[1,42,20,1]{3,0,2,1:T(1,128)}, f32[1,42,20,1]{3,0,2,1:T(1,128)}, u32[]{:S(2)}, u32[]{:S(2)}) collective-permute-start(f32[1,42,20,1]{3,0,2,1:T(1,128)} %get-tuple-element.52), channel_id=1, source_target_pairs={{4,0},{8,4},{12,8},{0,12},{5,1},{9,5},{13,9},{1,13},{6,2},{10,6},{... | collective-permute-start | bytes 10088 | tf_op jit(solution)/shard_map/ppermute | solution.py:29
  46.3 11.4 %collective-permute-start.3 = (f32[1,42,20,1]{3,0,2,1:T(1,128)}, f32[1,42,20,1]{3,0,2,1:T(1,128)}, u32[]{:S(2)}, u32[]{:S(2)}) collective-permute-start(f32[1,42,20,1]{3,0,2,1:T(1,128)} %get-tuple-element.53), channel_id=1, source_target_pairs={{0,4},{4,8},{8,12},{12,0},{1,5},{5,9},{9,13},{13,1},{2,6},{6,10},{... | collective-permute-start | bytes 10088 | tf_op jit(solution)/shard_map/ppermute | solution.py:28
  46.3 24.5 %copy-start.6 = (f32[20,512]{1,0:T(8,128)S(1)}, f32[20,512]{1,0:T(8,128)}, u32[]{:S(2)}) copy-start(f32[20,512]{1,0:T(8,128)} %copy-done.5) | copy-start | bytes 122884
  70.8 4.9 %copy-start.8 = (f32[1,20,512]{2,0,1:T(1,128)S(1)}, f32[1,20,512]{2,0,1:T(1,128)}, u32[]{:S(2)}) copy-start(f32[1,20,512]{2,0,1:T(1,128)} %param.15) | copy-start | bytes 122884
  81.7 3.5 %copy-start.10 = (s32[512,4]{0,1:T(4,128)S(1)}, s32[512,4]{0,1:T(4,128)}, u32[]{:S(2)}) copy-start(s32[512,4]{0,1:T(4,128)} %param.18) | copy-start | bytes 24580
  81.7 20.2 %copy-start.11 = (s32[512]{0:T(512)S(1)}, s32[512]{0:T(512)}, u32[]{:S(2)}) copy-start(s32[512]{0:T(512)} %param.19) | copy-start | bytes 6148
  81.7 20.3 %copy-start.9 = (f32[512,4]{0,1:T(4,128)S(1)}, f32[512,4]{0,1:T(4,128)}, u32[]{:S(2)}) copy-start(f32[512,4]{0,1:T(4,128)} %param.17) | copy-start | bytes 24580
  82.2 1.3 %copy-start.1 = (f32[1,42,20,512]{3,2,1,0:T(8,128)}, f32[1,42,20,512]{3,2,1,0:T(8,128)S(1)}, u32[]{:S(2)}) copy-start(f32[1,42,20,512]{3,2,1,0:T(8,128)S(1)} %copy_select_fusion) | copy-start | bytes 5160964
  83.5 4.1 %collective-permute-start.4 = (f32[20,512]{1,0:T(8,128)S(1)}, f32[20,512]{1,0:T(8,128)S(1)}, u32[]{:S(2)}, u32[]{:S(2)}) collective-permute-start(f32[20,512]{1,0:T(8,128)S(1)} %slice_bitcast_fusion), channel_id=1, source_target_pairs={{0,1},{1,0},{2,3},{3,2},{4,5},{5,4},{6,7},{7,6},{8,9},{9,8},{10,11... | collective-permute-start | bytes 122888 | tf_op jit(solution)/shard_map/ppermute | solution.py:13
  87.7 5.4 %collective-permute-start.5 = (f32[40,512]{1,0:T(8,128)S(1)}, f32[40,512]{1,0:T(8,128)S(1)}, u32[]{:S(2)}, u32[]{:S(2)}) collective-permute-start(f32[40,512]{1,0:T(8,128)S(1)} %maximum_select_fusion.2), channel_id=1, source_target_pairs={{0,2},{1,3},{2,0},{3,1},{4,6},{5,7},{6,4},{7,5},{8,10},{9,11},{10,... | collective-permute-start | bytes 245768 | tf_op jit(solution)/shard_map/ppermute | solution.py:13
  98.5 5.0 %collective-permute-start.6 = (f32[4,2048]{1,0:T(4,128)S(1)}, f32[4,2048]{1,0:T(4,128)S(1)}, u32[]{:S(2)}, u32[]{:S(2)}) collective-permute-start(f32[4,2048]{1,0:T(4,128)S(1)} %all_gather.3), channel_id=1, source_target_pairs={{0,16},{1,17},{2,18},{3,19},{4,20},{5,21},{6,22},{7,23},{8,24},{9,... | collective-permute-start | bytes 98312 | tf_op jit(solution)/shard_map/ppermute | solution.py:37
  103.9 11.7 %slice-start = ((f32[1,42,20,512]{3,2,1,0:T(8,128)}), f32[1,40,20,512]{3,2,1,0:T(8,128)S(1)}, s32[]{:S(2)}) async-start(f32[1,42,20,512]{3,2,1,0:T(8,128)} %copy-done.1), calls=%async_computation | async-start | bytes 3932160 | tf_op jit(solution)/shard_map/slice | solution.py:105
